TPU v7x, 32 devices: a whole 2x2x4 slice. The times are simulated.
32 devices in a mesh: pair: 2 (over x), blk: 8 (over z, y), group: 2 (over core).
Axes of the slice: x: 2, y: 2, z: 4, core: 2. Of those that a mesh axis runs over, the one named last changes fastest.
Arguments:
- codes: int32 [32, 1536, 256], P(('pair', 'blk', 'group')), may hold values from 0 to 255
- scales: int32 [32, 1536, 8], P(('pair', 'blk', 'group')), may hold values from -7 to 0
- inputs: bfloat16 [4096, 1536], P(('pair', 'blk', 'group')), may hold values from -6 to 6
- cotangent: bfloat16 [4096, 256], P(('pair', 'blk', 'group')), may hold values from -6 to 6
Outputs:
- earlier_grad: float32 [1536, 256], replicated
- current_grad: float32 [1536, 256], replicated
All inputs are finite; a program needn't handle non-finite values.
Results may differ from a plain program's by a relative error of at most 0.0003.
Values sent between devices are 32-bit elements; how exact they have to be, the bound alone decides.
No kernel may reach another device: no remote copies, remote signals or barrier semaphores. Data moves between devices by JAX's collectives and lax.ppermute only.
A program may use at most 64 MiB of HBM per device.

v0:
```python
import jax
import jax.numpy as jnp
from jax import lax
from jax.sharding import PartitionSpec as P


def decode(codes, scales):
    codes = codes[0]
    scales = scales[0]
    rows, width = codes.shape
    sign = 1.0 - 2.0 * (codes // 128).astype(jnp.float32)
    field = codes // 8 % 16
    mant = (codes % 8).astype(jnp.float32)
    frac = jnp.where(field > 0, 8.0 + mant, mant)
    power = jnp.where(field > 0, field, 1) - 10
    expo = power.reshape(rows, scales.shape[1], width // scales.shape[1]) + scales[:, :, None]
    return sign * frac * jnp.exp2(expo.reshape(rows, width).astype(jnp.float32))


def combine(stack, count):
    pooled = lax.psum(stack, "pair")
    share = lax.psum_scatter(pooled, "blk", scatter_dimension=1, tiled=True)
    total = lax.psum_scatter(share, "group", scatter_dimension=1, tiled=True) / count
    return lax.all_gather(total, ("blk", "group"), axis=1, tiled=True)


def key_product(inputs, cotangent):
    return lax.dot_general(
        inputs, cotangent, (((0,), (0,)), ((), ())), preferred_element_type=jnp.float32
    )


def local(codes, scales, inputs, cotangent):
    count = lax.axis_size("pair") * lax.axis_size("blk") * lax.axis_size("group")
    decoded = decode(codes, scales)
    product = key_product(inputs, cotangent)
    summed = combine(jnp.stack([decoded, product]), count)
    earlier_grad = summed[0]
    current_grad = summed[1]
    return (earlier_grad, current_grad)


def solution(mesh):
    in_specs = (
        P(("pair", "blk", "group"), None, None),
        P(("pair", "blk", "group"), None, None),
        P(("pair", "blk", "group"), None),
        P(("pair", "blk", "group"), None),
    )
    out_specs = (P(), P())
    return jax.shard_map(local, mesh=mesh, in_specs=in_specs, out_specs=out_specs, check_vma=False)
```

profile of v0, /device:TPU:0, one launch (start us, length us, event | category | flops | bytes accessed | tf_op | source)
XLA Modules:
  0.0 186.2 jit_solution(1373778970033017761)
XLA Ops:
  7.2 0.0 copy-start
  7.2 0.0 reduce-scatter.3.cloned.1.call-start
  7.2 1.0 add.58
  8.2 0.5 copy.7
  8.7 0.0 copy-start.1
  8.7 4.5 %fusion.5 = f32[1,1536,256]{2,1,0:T(8,128)S(1)} fusion(s32[1,1536,256]{2,1,0:T(8,128)S(1)} %copy.7, s32[1,1536,256]{2,1,0:T(8,128)} %param.4), kind=kLoop, calls=%fused_computation.20 | loop fusion | flops 21233664 | bytes 4718592 | tf_op jit(solution)/shard_map/mul | solution.py:17
  13.2 0.0 copy-done
  13.2 0.0 copy-done.1
  13.3 0.4 convolution_bitcast_fusion
  13.6 1.9 pad_maximum_fusion
  15.5 0.0 reduce-scatter.3.cloned.1.call-update
  15.5 0.0 reduce-scatter.5.cloned.1.call-start
  15.6 77.1 %reduce-scatter.3.cloned.1.call-done = f32[2,192,256]{2,1,0:T(8,128)} async-done(((f32[2,1536,256]{2,1,0:T(8,128)}), f32[2,192,256]{2,1,0:T(8,128)}) %reduce-scatter.3.cloned.1.call-update) | async-done | bytes 393232 | tf_op jit(solution)/shard_map/reduce_scatter | solution.py:22
  92.7 0.0 reduce-scatter.5.cloned.1.call-update
  92.7 0.0 all-reduce.2.cloned.1.call-start
  92.8 9.1 %reduce-scatter.5.cloned.1.call-done = f32[2,96,256]{2,1,0:T(8,128)} async-done(((f32[2,192,256]{2,1,0:T(8,128)}), f32[2,96,256]{2,1,0:T(8,128)}) %reduce-scatter.5.cloned.1.call-update) | async-done | bytes 196624 | tf_op jit(solution)/shard_map/reduce_scatter | solution.py:23
  101.9 0.0 all-reduce.2.cloned.1.call-update
  101.9 0.0 all-gather.2.cloned.1.call-start
  102.0 25.8 %all-reduce.2.cloned.1.call-done = f32[2,96,256]{2,1,0:T(8,128)} async-done(((f32[2,96,256]{2,1,0:T(8,128)}), f32[2,96,256]{2,1,0:T(8,128)}) %all-reduce.2.cloned.1.call-update) | async-done | bytes 196624 | tf_op jit(solution)/shard_map/psum | solution.py:21
  127.7 1.6 broadcast_multiply_fusion
  129.3 0.0 all-gather.2.cloned.1.call-update
  129.4 46.6 %all-gather.2.cloned.1.call-done = f32[2,1536,256]{2,1,0:T(8,128)} async-done(((f32[2,96,256]{2,1,0:T(8,128)}), f32[2,1536,256]{2,1,0:T(8,128)}) %all-gather.2.cloned.1.call-update) | async-done | bytes 3145744 | tf_op jit(solution)/shard_map/all_gather | solution.py:24
  176.0 3.7 %slice_bitcast_fusion = (f32[1536,256]{1,0:T(8,128)}, f32[1536,256]{1,0:T(8,128)}) fusion(f32[2,1536,256]{2,1,0:T(8,128)} %all-gather.2.cloned.1.call-done), kind=kLoop, calls=%fused_computation.28 | loop fusion | bytes 6291456 | tf_op jit(solution)/shard_map/squeeze | solution.py:39
Async XLA Ops:
  7.2 6.1 %copy-start = (bf16[128,1536]{1,0:T(8,128)(2,1)S(1)}, bf16[128,1536]{1,0:T(8,128)(2,1)}, u32[]{:S(2)}) copy-start(bf16[128,1536]{1,0:T(8,128)(2,1)} %param.6) | copy-start | bytes 1179652
  7.2 85.5 %reduce-scatter.3.cloned.1.call-start = ((), (), s32[]{:S(2)}) async-start(), calls=%async_computation.3 | async-start | bytes 3538944 | tf_op jit(solution)/shard_map/reduce_scatter | solution.py:22
  8.7 4.5 %copy-start.1 = (bf16[128,256]{1,0:T(8,128)(2,1)S(1)}, bf16[128,256]{1,0:T(8,128)(2,1)}, u32[]{:S(2)}) copy-start(bf16[128,256]{1,0:T(8,128)(2,1)} %param.7) | copy-start | bytes 196612
  15.5 86.4 %reduce-scatter.5.cloned.1.call-start = ((), (), s32[]{:S(2)}) async-start(), calls=%async_computation.4 | async-start | bytes 589824 | tf_op jit(solution)/shard_map/reduce_scatter | solution.py:23
  92.7 35.0 %all-reduce.2.cloned.1.call-start = ((), (), s32[]{:S(2)}) async-start(), calls=%async_computation.5 | async-start | bytes 393216 | tf_op jit(solution)/shard_map/psum | solution.py:21
  101.9 74.0 %all-gather.2.cloned.1.call-start = ((), (), s32[]{:S(2)}) async-start(), calls=%async_computation.2 | async-start | bytes 3342336 | tf_op jit(solution)/shard_map/all_gather | solution.py:24
Sparse Core Ops, SparseCore 0:
  15.7 77.0 reduce-scatter.2
  94.9 6.8 reduce-scatter.4
  104.2 23.5 all-reduce.1
  130.4 45.4 all-gather.1
where the time goes:
time: 186 us
  waiting for transfers between devices  159 us (85%)
  between operations  13.8 us (7%)
  other arithmetic  7.97 us (4%)
  local copies, waits for them, and re-layouts  5.23 us (3%)
    reduce_scatter x1, waiting for transfers between devices, combine(): share = lax.psum_scatter(pooled, 'blk', scatter_dimension=1, tiled=True)  77.1 us
    all_gather x1, waiting for transfers between devices, combine(): return lax.all_gather(total, ('blk', 'group'), axis=1, tiled=True)  46.6 us
    psum x1, waiting for transfers between devices, combine(): pooled = lax.psum(stack, 'pair')  25.8 us
    reduce_scatter x1, waiting for transfers between devices, combine(): lax.psum_scatter(share, 'group', scatter_dimension=1, tiled=True) / count  9.11 us
    mul x1, other arithmetic, decode(): return sign * frac * jnp.exp2(expo.reshape(rows, width).astype(jnp.float32))  4.5 us
    squeeze x1, local copies, waits for them, and re-layouts, local(): current_grad = summed[1]  3.74 us
  transfers between devices with their start and end apart: 4, of which 4 were waited for; matrix products, arithmetic and copies ran while one was open for 0% of the time, Pallas kernels for 0%

commit v1 on v0

--- a/solution.py
+++ b/solution.py
@@ -18,7 +18,7 @@
 
 
 def combine(stack, count):
-    pooled = lax.psum(stack, "pair")
+    pooled = jnp.sum(lax.all_gather(stack, "pair"), axis=0)
     share = lax.psum_scatter(pooled, "blk", scatter_dimension=1, tiled=True)
     total = lax.psum_scatter(share, "group", scatter_dimension=1, tiled=True) / count
     return lax.all_gather(total, ("blk", "group"), axis=1, tiled=True)

time: 186 us -> 248 us (1.33)
  waiting for transfers between devices: 159 us -> 214 us
  other arithmetic: 7.97 us -> 13.3 us
    all_gather x0 -> x1, waiting for transfers between devices: none -> 83.2 us  [combine(): pooled = jnp.sum(lax.all_gather(stack, 'pair'), axis=0)]
    psum x1 -> x0, waiting for transfers between devices: 25.8 us -> none  [combine(): pooled = lax.psum(stack, 'pair')]
    reduce_sum x0 -> x1, other arithmetic: none -> 5.3 us  [combine(): pooled = jnp.sum(lax.all_gather(stack, 'pair'), axis=0)]
    reduce_scatter x1, waiting for transfers between devices: 77.1 us -> 74.4 us  [combine(): share = lax.psum_scatter(pooled, 'blk', scatter_dimension=1, tiled=True)]
where the time goes in v1:
time: 248 us; the launch traced here: 247 us
  waiting for transfers between devices  214 us (86%)
  between operations  13.8 us (6%)
  other arithmetic  13.3 us (5%)
  local copies, waits for them, and re-layouts  5.23 us (2%)
    all_gather x1, waiting for transfers between devices, combine(): pooled = jnp.sum(lax.all_gather(stack, 'pair'), axis=0)  83.2 us
    reduce_scatter x1, waiting for transfers between devices, combine(): share = lax.psum_scatter(pooled, 'blk', scatter_dimension=1, tiled=True)  74.4 us
    all_gather x1, waiting for transfers between devices, combine(): return lax.all_gather(total, ('blk', 'group'), axis=1, tiled=True)  47.7 us
    reduce_scatter x1, waiting for transfers between devices, combine(): lax.psum_scatter(share, 'group', scatter_dimension=1, tiled=True) / count  9.12 us
    reduce_sum x1, other arithmetic, combine(): pooled = jnp.sum(lax.all_gather(stack, 'pair'), axis=0)  5.3 us
  transfers between devices with their start and end apart: 4, of which 4 were waited for; matrix products, arithmetic and copies ran while one was open for 0% of the time, Pallas kernels for 0%

profile of v1, /device:TPU:0, one launch (start us, length us, event | category | flops | bytes accessed | tf_op | source)
XLA Modules:
  0.0 247.4 jit_solution(6054982789926673420)
XLA Ops:
  7.2 0.0 copy-start
  7.2 0.0 all-gather.6.cloned.1.call-start
  7.2 1.0 add.56
  8.2 0.5 copy.8
  8.7 0.0 copy-start.1
  8.7 4.5 %fusion.5 = f32[1,1536,256]{2,1,0:T(8,128)S(1)} fusion(s32[1,1536,256]{2,1,0:T(8,128)S(1)} %copy.8, s32[1,1536,256]{2,1,0:T(8,128)} %param.4), kind=kLoop, calls=%fused_computation.20 | loop fusion | flops 21233664 | bytes 4718592 | tf_op jit(solution)/shard_map/mul | solution.py:17
  13.2 0.0 copy-done
  13.2 0.0 copy-done.1
  13.3 0.4 convolution_bitcast_fusion
  13.6 1.9 pad_maximum_fusion
  15.6 0.0 all-gather.6.cloned.1.call-update
  15.6 0.0 reduce-scatter.3.cloned.1.call-start
  15.6 83.2 %all-gather.6.cloned.1.call-done = f32[4,1536,256]{2,1,0:T(8,128)} async-done(((f32[2,1536,256]{2,1,0:T(8,128)}), f32[4,1536,256]{2,1,0:T(8,128)}) %all-gather.6.cloned.1.call-update) | async-done | bytes 6291472 | tf_op jit(solution)/shard_map/all_gather | solution.py:21
  98.8 5.3 %reduce_sum.9 = f32[2,1536,256]{2,1,0:T(8,128)} reduce(f32[2,2,1536,256]{3,2,1,0:T(8,128)} %bitcast.11, f32[]{:T(128)} %constant.65.clone.1), dimensions={0}, to_apply=%region_0.1 | reduce | flops 786432 | bytes 9437188 | tf_op jit(solution)/shard_map/reduce_sum | solution.py:21
  104.1 0.0 reduce-scatter.3.cloned.1.call-update
  104.1 0.0 reduce-scatter.5.cloned.1.call-start
  104.2 74.4 %reduce-scatter.3.cloned.1.call-done = f32[2,192,256]{2,1,0:T(8,128)} async-done(((f32[2,1536,256]{2,1,0:T(8,128)}), f32[2,192,256]{2,1,0:T(8,128)}) %reduce-scatter.3.cloned.1.call-update) | async-done | bytes 393232 | tf_op jit(solution)/shard_map/reduce_scatter | solution.py:22
  178.6 0.0 reduce-scatter.5.cloned.1.call-update
  178.6 0.0 all-gather.4.cloned.1.call-start
  178.7 9.1 %reduce-scatter.5.cloned.1.call-done = f32[2,96,256]{2,1,0:T(8,128)} async-done(((f32[2,192,256]{2,1,0:T(8,128)}), f32[2,96,256]{2,1,0:T(8,128)}) %reduce-scatter.5.cloned.1.call-update) | async-done | bytes 196624 | tf_op jit(solution)/shard_map/reduce_scatter | solution.py:23
  187.8 1.6 broadcast_multiply_fusion
  189.4 0.0 all-gather.4.cloned.1.call-update
  189.4 47.7 %all-gather.4.cloned.1.call-done = f32[2,1536,256]{2,1,0:T(8,128)} async-done(((f32[2,96,256]{2,1,0:T(8,128)}), f32[2,1536,256]{2,1,0:T(8,128)}) %all-gather.4.cloned.1.call-update) | async-done | bytes 3145744 | tf_op jit(solution)/shard_map/all_gather | solution.py:24
  237.1 3.7 %slice_bitcast_fusion = (f32[1536,256]{1,0:T(8,128)}, f32[1536,256]{1,0:T(8,128)}) fusion(f32[2,1536,256]{2,1,0:T(8,128)} %all-gather.4.cloned.1.call-done), kind=kLoop, calls=%fused_computation.28 | loop fusion | bytes 6291456 | tf_op jit(solution)/shard_map/squeeze | solution.py:39
Async XLA Ops:
  7.2 6.1 %copy-start = (bf16[128,1536]{1,0:T(8,128)(2,1)S(1)}, bf16[128,1536]{1,0:T(8,128)(2,1)}, u32[]{:S(2)}) copy-start(bf16[128,1536]{1,0:T(8,128)(2,1)} %param.6) | copy-start | bytes 1179652
  7.2 91.6 %all-gather.6.cloned.1.call-start = ((), (), s32[]{:S(2)}) async-start(), calls=%async_computation.5 | async-start | bytes 9437184 | tf_op jit(solution)/shard_map/all_gather | solution.py:21
  8.7 4.5 %copy-start.1 = (bf16[128,256]{1,0:T(8,128)(2,1)S(1)}, bf16[128,256]{1,0:T(8,128)(2,1)}, u32[]{:S(2)}) copy-start(bf16[128,256]{1,0:T(8,128)(2,1)} %param.7) | copy-start | bytes 196612
  15.6 163.0 %reduce-scatter.3.cloned.1.call-start = ((), (), s32[]{:S(2)}) async-start(), calls=%async_computation.2 | async-start | bytes 3538944 | tf_op jit(solution)/shard_map/reduce_scatter | solution.py:22
  104.1 83.7 %reduce-scatter.5.cloned.1.call-start = ((), (), s32[]{:S(2)}) async-start(), calls=%async_computation.3 | async-start | bytes 589824 | tf_op jit(solution)/shard_map/reduce_scatter | solution.py:23
  178.6 58.5 %all-gather.4.cloned.1.call-start = ((), (), s32[]{:S(2)}) async-start(), calls=%async_computation.4 | async-start | bytes 3342336 | tf_op jit(solution)/shard_map/all_gather | solution.py:24
Sparse Core Ops, SparseCore 0:
  15.7 83.0 all-gather.5
  104.3 74.2 reduce-scatter.2
  180.8 6.8 reduce-scatter.4
  190.5 46.5 all-gather.3
